TPU v7x, 32 devices: a whole 2x2x4 slice. The times are simulated.
32 devices in a mesh: blk: 8 (over y, x, core), rows: 4 (over z).
Axes of the slice: x: 2, y: 2, z: 4, core: 2. Of those that a mesh axis runs over, the one named last changes fastest.
Arguments:
- sens_tiles: bfloat16 [2048, 512, 128], P('blk', 'rows'), may hold values from -1 to 1
- start_basis: bfloat16 [64, 32768], P(None, 'blk'), may hold values from -6 to 6
- row_blocks: int32 [2048, 4], P('blk', 'rows'), may hold values from 0 to 7, as said below
- col_blocks: int32 [2048, 4], P('blk', 'rows'), may hold values from 0 to 31, as said below
- live_counts: int32 [8, 4], P('blk', 'rows'), may hold values from 64 to 256, as said below
Outputs:
- orthonormal: float32 [4, 64, 32768], P(None, None, ('blk', 'rows'))
Inputs may be any that keep to these rules, and one draw needn't show every extreme that they name: Within one device the pairs (row_blocks, col_blocks) of its 256 slots are distinct. Within one device the pairs (row_blocks, col_blocks) of its 256 slots are distinct. Slots 0 to live_counts - 1 of a device hold its tiles; some device has all 256 slots live.
All inputs are finite; a program needn't handle non-finite values.
Results may differ from a plain program's by a relative error of at most 0.012.
The roundings to bfloat16 on the way count: a program that leaves them out, or rounds other values in their place, can miss the bound.
Values may be sent and summed in bfloat16 or wider, within the bound.
A program may use at most 128 MiB of HBM per device.

v0:
```python
import jax
import jax.numpy as jnp
from jax import lax
from jax.sharding import PartitionSpec as P

RB = 8
CB = 32
ITERS = 4


def apply_forward(sens_tiles, basis_now, col_slots, row_onehot):
    vectors = basis_now.shape[0]
    tile_size = sens_tiles.shape[2]
    picked = jnp.take(basis_now.reshape(vectors, CB, tile_size), col_slots, axis=1)
    products = jnp.einsum("kst,sit->ksi", picked, sens_tiles, preferred_element_type=jnp.float32)
    summed = jnp.einsum("ksi,rs->kri", products, row_onehot, precision=lax.Precision.HIGHEST)
    return summed.reshape(vectors, RB * tile_size)


def apply_backward(sens_tiles, image_half, row_slots, col_onehot):
    vectors = image_half.shape[0]
    tile_size = sens_tiles.shape[2]
    picked = jnp.take(image_half.reshape(vectors, RB, tile_size), row_slots, axis=1)
    products = jnp.einsum("ksi,sij->ksj", picked, sens_tiles, preferred_element_type=jnp.float32)
    summed = jnp.einsum("ksj,cs->kcj", products, col_onehot, precision=lax.Precision.HIGHEST)
    return summed.reshape(vectors, CB * tile_size)


def factor_whole(current, total):
    local_gram = jnp.dot(current, current.T, precision=lax.Precision.HIGHEST)
    gram = lax.psum(local_gram, "blk") / total
    lower = jnp.linalg.cholesky(gram)
    return jax.scipy.linalg.solve_triangular(lower, current, lower=True)


def local(sens_tiles, start_basis, row_blocks, col_blocks, live_counts):
    row_slots = row_blocks[:, 0]
    col_slots = col_blocks[:, 0]
    count_live = live_counts[0, 0]
    slot_total = sens_tiles.shape[0]
    tile_size = sens_tiles.shape[2]
    live = jnp.arange(slot_total) < count_live
    row_onehot = ((row_slots[None, :] == jnp.arange(RB)[:, None]) & live[None, :]).astype(
        jnp.float32
    )
    col_onehot = ((col_slots[None, :] == jnp.arange(CB)[:, None]) & live[None, :]).astype(
        jnp.float32
    )
    total = float(CB * tile_size * lax.axis_size("blk"))
    own_width = CB * tile_size // lax.axis_size("rows")
    basis_now = start_basis
    results = []
    for iteration in range(ITERS):
        partial_image = apply_forward(sens_tiles, basis_now, col_slots, row_onehot)
        image = lax.psum(partial_image, "blk")
        image_half = image.astype(jnp.bfloat16)
        partial_hessian = apply_backward(sens_tiles, image_half, row_slots, col_onehot)
        hessian = lax.psum(partial_hessian, "rows")
        whole_result = factor_whole(hessian, total)
        basis_now = whole_result.astype(jnp.bfloat16)
        result = lax.dynamic_slice_in_dim(
            whole_result, lax.axis_index("rows") * own_width, own_width, 1
        )
        results.append(result)
    return jnp.stack(results, axis=0)


def solution(mesh):
    in_specs = (
        P("blk", "rows", None),
        P(None, "blk"),
        P("blk", "rows"),
        P("blk", "rows"),
        P("blk", "rows"),
    )
    out_specs = P(None, None, ("blk", "rows"))
    return jax.shard_map(local, mesh=mesh, in_specs=in_specs, out_specs=out_specs, check_vma=False)
```

profile of v0, /device:TPU:0, one launch (start us, length us, event | category | flops | bytes accessed | tf_op | source)
XLA Modules:
  0.0 653.3 jit_solution(9419659961309902612)
XLA Ops:
  12.5 10.4 %fusion.48 = f32[64,256,128]{2,0,1:T(8,128)S(1)} fusion(bf16[256,128,128]{2,1,0:T(8,128)(2,1)} %param.12, bf16[256,64,128]{2,1,0:T(8,128)(2,1)} %gather_fusion, pred[256]{0:T(512)(128)(4,1)S(1)} %get-tuple-element.8), kind=kOutput, calls=%fused_computation.56 | convolution fusion | flops 538968064 | bytes 20971776 | tf_op jit(solution)/shard_map/kst,sit->ksi/dot_general | solution.py:15
  22.9 7.5 %fusion.14 = f32[8,64,128]{2,0,1:T(8,128)S(1)} fusion(f32[64,256,128]{2,0,1:T(8,128)S(1)} %fusion.48, s32[256]{0:T(256)S(1)} %bitcast.242, pred[256]{0:T(512)(128)(4,1)S(1)} %iota_compare_fusion.4), kind=kOutput, calls=%fused_computation.22 | convolution fusion | flops 201330688 | bytes 8652032 | tf_op jit(solution)/shard_map/ksi,rs->kri/dot_general | solution.py:16
  30.8 28.4 %all-reduce.16 = bf16[64,1024]{1,0:T(8,128)(2,1)S(1)} all-reduce(f32[64,1024]{1,0:T(8,128)S(1)} %bitcast.236), channel_id=1, replica_groups=mesh['blk'=8,'rows'=4] {'blk'}, use_global_device_ids=true, to_apply=%region_0.0 | all-reduce | flops 65536 | bytes 393216 | tf_op jit(solution)/shard_map/psum | solution.py:55
  69.4 7.7 %fusion.12 = f32[32,64,128]{2,0,1:T(8,128)S(1)} fusion(f32[64,256,128]{2,0,1:T(8,128)S(1)} %fusion.51, s32[256]{0:T(256)S(1)} %bitcast.248, pred[256]{0:T(512)(128)(4,1)S(1)} %iota_compare_fusion.4), kind=kOutput, calls=%fused_computation.20 | convolution fusion | flops 805322752 | bytes 9438464 | tf_op jit(solution)/shard_map/ksj,cs->kcj/dot_general | solution.py:25
  78.7 51.6 %all-reduce.9.cloned.1.call-done = f32[64,4096]{1,0:T(8,128)} async-done(((f32[64,4096]{1,0:T(8,128)}), f32[64,4096]{1,0:T(8,128)}) %all-reduce.9.cloned.1.call-update) | async-done | bytes 1048592 | tf_op jit(solution)/shard_map/psum | solution.py:58
  132.8 24.3 %psum.86 = f32[64,64]{0,1:T(8,128)S(1)} all-reduce(f32[64,64]{0,1:T(8,128)S(1)} %fusion.116), channel_id=1, replica_groups=mesh['blk'=8,'rows'=4] {'blk'}, use_global_device_ids=true, to_apply=%region_2.0 | all-reduce | flops 4096 | bytes 32768 | tf_op jit(solution)/shard_map/psum | solution.py:31
  175.7 10.4 %fusion.54 = f32[64,256,128]{2,0,1:T(8,128)S(1)} fusion(bf16[256,128,128]{2,1,0:T(8,128)(2,1)} %param.12, bf16[256,64,128]{2,1,0:T(8,128)(2,1)} %gather_fusion.2, pred[256]{0:T(512)(128)(4,1)S(1)} %get-tuple-element.8), kind=kOutput, calls=%fused_computation.58 | convolution fusion | flops 538968064 | bytes 20971776 | tf_op jit(solution)/shard_map/kst,sit->ksi/dot_general | solution.py:15
  186.1 7.9 %fusion.10 = f32[8,64,128]{2,0,1:T(8,128)S(1)} fusion(f32[64,256,128]{2,0,1:T(8,128)S(1)} %fusion.54, s32[256]{0:T(256)S(1)} %bitcast.243, pred[256]{0:T(512)(128)(4,1)S(1)} %iota_compare_fusion.4), kind=kOutput, calls=%fused_computation.18 | convolution fusion | flops 201330688 | bytes 8652032 | tf_op jit(solution)/shard_map/ksi,rs->kri/dot_general | solution.py:16
  194.0 25.3 %all-reduce.17 = bf16[64,1024]{1,0:T(8,128)(2,1)S(1)} all-reduce(f32[64,1024]{1,0:T(8,128)S(1)} %bitcast.237), channel_id=1, replica_groups=mesh['blk'=8,'rows'=4] {'blk'}, use_global_device_ids=true, to_apply=%region_5.10 | all-reduce | flops 65536 | bytes 393216 | tf_op jit(solution)/shard_map/psum | solution.py:55
  229.4 7.7 %fusion.8 = f32[32,64,128]{2,0,1:T(8,128)S(1)} fusion(f32[64,256,128]{2,0,1:T(8,128)S(1)} %fusion.57, s32[256]{0:T(256)S(1)} %bitcast.249, pred[256]{0:T(512)(128)(4,1)S(1)} %iota_compare_fusion.4), kind=kOutput, calls=%fused_computation.16 | convolution fusion | flops 805322752 | bytes 9438464 | tf_op jit(solution)/shard_map/ksj,cs->kcj/dot_general | solution.py:25
  238.8 49.5 %all-reduce.11.cloned.1.call-done = f32[64,4096]{1,0:T(8,128)} async-done(((f32[64,4096]{1,0:T(8,128)}), f32[64,4096]{1,0:T(8,128)}) %all-reduce.11.cloned.1.call-update) | async-done | bytes 1048592 | tf_op jit(solution)/shard_map/psum | solution.py:58
  290.7 24.3 %psum.89 = f32[64,64]{0,1:T(8,128)S(1)} all-reduce(f32[64,64]{0,1:T(8,128)S(1)} %fusion.117), channel_id=1, replica_groups=mesh['blk'=8,'rows'=4] {'blk'}, use_global_device_ids=true, to_apply=%region_7.12 | all-reduce | flops 4096 | bytes 32768 | tf_op jit(solution)/shard_map/psum | solution.py:31
  333.6 10.4 %fusion.60 = f32[64,256,128]{2,0,1:T(8,128)S(1)} fusion(bf16[256,128,128]{2,1,0:T(8,128)(2,1)} %param.12, bf16[256,64,128]{2,1,0:T(8,128)(2,1)} %gather_fusion.4, pred[256]{0:T(512)(128)(4,1)S(1)} %get-tuple-element.8), kind=kOutput, calls=%fused_computation.60 | convolution fusion | flops 538968064 | bytes 20971776 | tf_op jit(solution)/shard_map/kst,sit->ksi/dot_general | solution.py:15
  344.0 7.9 %fusion.6 = f32[8,64,128]{2,0,1:T(8,128)S(1)} fusion(f32[64,256,128]{2,0,1:T(8,128)S(1)} %fusion.60, s32[256]{0:T(256)S(1)} %bitcast.244, pred[256]{0:T(512)(128)(4,1)S(1)} %iota_compare_fusion.4), kind=kOutput, calls=%fused_computation.14 | convolution fusion | flops 201330688 | bytes 8652032 | tf_op jit(solution)/shard_map/ksi,rs->kri/dot_general | solution.py:16
  352.0 25.3 %all-reduce.18 = bf16[64,1024]{1,0:T(8,128)(2,1)S(1)} all-reduce(f32[64,1024]{1,0:T(8,128)S(1)} %bitcast.238), channel_id=1, replica_groups=mesh['blk'=8,'rows'=4] {'blk'}, use_global_device_ids=true, to_apply=%region_8.13 | all-reduce | flops 65536 | bytes 393216 | tf_op jit(solution)/shard_map/psum | solution.py:55
  387.3 7.7 %fusion.4 = f32[32,64,128]{2,0,1:T(8,128)S(1)} fusion(f32[64,256,128]{2,0,1:T(8,128)S(1)} %fusion.63, s32[256]{0:T(256)S(1)} %bitcast.250, pred[256]{0:T(512)(128)(4,1)S(1)} %iota_compare_fusion.4), kind=kOutput, calls=%fused_computation.12 | convolution fusion | flops 805322752 | bytes 9438464 | tf_op jit(solution)/shard_map/ksj,cs->kcj/dot_general | solution.py:25
  396.7 49.5 %all-reduce.13.cloned.1.call-done = f32[64,4096]{1,0:T(8,128)} async-done(((f32[64,4096]{1,0:T(8,128)}), f32[64,4096]{1,0:T(8,128)}) %all-reduce.13.cloned.1.call-update) | async-done | bytes 1048592 | tf_op jit(solution)/shard_map/psum | solution.py:58
  448.7 24.2 %psum.92 = f32[64,64]{0,1:T(8,128)S(1)} all-reduce(f32[64,64]{0,1:T(8,128)S(1)} %fusion.118), channel_id=1, replica_groups=mesh['blk'=8,'rows'=4] {'blk'}, use_global_device_ids=true, to_apply=%region_10.15 | all-reduce | flops 4096 | bytes 32768 | tf_op jit(solution)/shard_map/psum | solution.py:31
  491.6 10.4 %fusion.66 = f32[64,256,128]{2,0,1:T(8,128)S(1)} fusion(bf16[256,128,128]{2,1,0:T(8,128)(2,1)} %param.12, bf16[256,64,128]{2,1,0:T(8,128)(2,1)} %gather_fusion.6, pred[256]{0:T(512)(128)(4,1)S(1)} %get-tuple-element.8), kind=kOutput, calls=%fused_computation.62 | convolution fusion | flops 538968064 | bytes 20971776 | tf_op jit(solution)/shard_map/kst,sit->ksi/dot_general | solution.py:15
  501.9 7.7 %fusion.2 = f32[8,64,128]{2,0,1:T(8,128)S(1)} fusion(f32[64,256,128]{2,0,1:T(8,128)S(1)} %fusion.66, s32[256]{0:T(256)S(1)} %bitcast.245, pred[256]{0:T(512)(128)(4,1)S(1)} %iota_compare_fusion.4), kind=kOutput, calls=%fused_computation.10 | convolution fusion | flops 201330688 | bytes 8652032 | tf_op jit(solution)/shard_map/ksi,rs->kri/dot_general | solution.py:16
  509.7 25.3 %all-reduce.19 = bf16[64,1024]{1,0:T(8,128)(2,1)S(1)} all-reduce(f32[64,1024]{1,0:T(8,128)S(1)} %bitcast.239), channel_id=1, replica_groups=mesh['blk'=8,'rows'=4] {'blk'}, use_global_device_ids=true, to_apply=%region_11.16 | all-reduce | flops 65536 | bytes 393216 | tf_op jit(solution)/shard_map/psum | solution.py:55
  545.1 7.7 %fusion = f32[32,64,128]{2,0,1:T(8,128)S(1)} fusion(f32[64,256,128]{2,0,1:T(8,128)S(1)} %fusion.69, s32[256]{0:T(256)S(1)} %bitcast.251, pred[256]{0:T(512)(128)(4,1)S(1)} %iota_compare_fusion.4), kind=kOutput, calls=%fused_computation.8 | convolution fusion | flops 805322752 | bytes 9438464 | tf_op jit(solution)/shard_map/ksj,cs->kcj/dot_general | solution.py:25
  557.4 46.5 %all-reduce.15.cloned.1.call-done = f32[64,4096]{1,0:T(8,128)} async-done(((f32[64,4096]{1,0:T(8,128)}), f32[64,4096]{1,0:T(8,128)}) %all-reduce.15.cloned.1.call-update) | async-done | bytes 1048592 | tf_op jit(solution)/shard_map/psum | solution.py:58
  606.7 24.1 %psum.95 = f32[64,64]{0,1:T(8,128)S(1)} all-reduce(f32[64,64]{0,1:T(8,128)S(1)} %fusion.119), channel_id=1, replica_groups=mesh['blk'=8,'rows'=4] {'blk'}, use_global_device_ids=true, to_apply=%region_13.18 | all-reduce | flops 4096 | bytes 32768 | tf_op jit(solution)/shard_map/psum | solution.py:31
  (101 shorter events, 137.2 us)
Async XLA Ops:
  6.5 2.8 copy-start
  6.5 123.8 %all-reduce.9.cloned.1.call-start = ((), (), s32[]{:S(2)}) async-start(), calls=%async_computation | async-start | bytes 2097152 | tf_op jit(solution)/shard_map/psum | solution.py:58
  12.5 10.4 %copy-start.5 = (s32[256,1]{0,1:T(1,128)S(1)}, s32[256,1]{0,1:T(1,128)}, u32[]{:S(2)}) copy-start(s32[256,1]{0,1:T(1,128)} %param.14) | copy-start | bytes 3076
  62.3 7.0 %copy-start.6 = (s32[256,1]{0,1:T(1,128)S(1)}, s32[256,1]{0,1:T(1,128)}, u32[]{:S(2)}) copy-start(s32[256,1]{0,1:T(1,128)} %param.15) | copy-start | bytes 3076
  78.7 209.5 %all-reduce.11.cloned.1.call-start = ((), (), s32[]{:S(2)}) async-start(), calls=%async_computation.1 | async-start | bytes 2097152 | tf_op jit(solution)/shard_map/psum | solution.py:58
  171.6 1.0 copy-start.2
  238.7 207.5 %all-reduce.13.cloned.1.call-start = ((), (), s32[]{:S(2)}) async-start(), calls=%async_computation.2 | async-start | bytes 2097152 | tf_op jit(solution)/shard_map/psum | solution.py:58
  329.5 1.0 copy-start.3
  396.7 207.2 %all-reduce.15.cloned.1.call-start = ((), (), s32[]{:S(2)}) async-start(), calls=%async_computation.3 | async-start | bytes 2097152 | tf_op jit(solution)/shard_map/psum | solution.py:58
  487.4 1.0 copy-start.4
  554.4 91.9 %copy-start.1 = (bf16[64,4096]{1,0:T(8,128)(2,1)S(1)}, bf16[64,4096]{1,0:T(8,128)(2,1)}, u32[]{:S(2)}) copy-start(bf16[64,4096]{1,0:T(8,128)(2,1)} %param.13) | copy-start | bytes 1572868
Sparse Core Ops, SparseCore 0:
  78.8 51.4 all-reduce.8
  238.8 49.3 all-reduce.10
  396.8 49.3 all-reduce.12
  554.5 49.3 all-reduce.14
where the time goes:
time: 663 us; the launch traced here: 653 us
  blocking collectives  201 us (30%)
  waiting for transfers between devices  197 us (30%)
  matrix products  151 us (23%)
  other arithmetic  51.9 us (8%)
  local copies, waits for them, and re-layouts  37.5 us (6%)
  between operations  14.7 us (2%)
    psum x4, waiting for transfers between devices, local(): hessian = lax.psum(partial_hessian, 'rows')  197 us
    psum x4, blocking collectives, local(): image = lax.psum(partial_image, 'blk')  104 us
    psum x4, blocking collectives, factor_whole(): gram = lax.psum(local_gram, 'blk') / total  96.9 us
    dot_general x4, matrix products, apply_forward(): jnp.einsum('kst,sit->ksi', picked, sens_tiles, preferred_element_type=jnp...  41.5 us
    dot_general x4, matrix products, apply_forward(): jnp.einsum('ksi,rs->kri', products, row_onehot, precision=lax.Precision.H...  31 us
    dot_general x4, matrix products, apply_backward(): jnp.einsum('ksj,cs->kcj', products, col_onehot, precision=lax.Precision.H...  30.9 us
    dot_general x4, matrix products, apply_backward(): jnp.einsum('ksi,sij->ksj', picked, sens_tiles, preferred_element_type=jnp...  28.1 us
    another operation x12, other arithmetic, factor_whole(): lower = jnp.linalg.cholesky(gram)  26.1 us
  transfers between devices with their start and end apart: 4, of which 4 were waited for; matrix products, arithmetic and copies ran while one was open for 0% of the time, Pallas kernels for 0%

commit v1 on v0

--- a/solution.py
+++ b/solution.py
@@ -2,10 +2,22 @@
 import jax.numpy as jnp
 from jax import lax
 from jax.sharding import PartitionSpec as P
+from jax.lax import axis_size, ppermute
 
 RB = 8
 CB = 32
 ITERS = 4
+
+
+def node_time(xs, mesh_name):
+    parts_n = axis_size(mesh_name)
+    parts_out = xs
+    clean = lambda s_next: [(kk, kk ^ s_next) for kk in range(parts_n)]
+    for i0 in range(parts_n.bit_length() - 1):
+        left_arr = clean(1 << i0)
+        d_next = ppermute(parts_out, mesh_name, left_arr)
+        parts_out = parts_out + d_next
+    return parts_out
 
 
 def apply_forward(sens_tiles, basis_now, col_slots, row_onehot):
@@ -55,7 +67,7 @@
         image = lax.psum(partial_image, "blk")
         image_half = image.astype(jnp.bfloat16)
         partial_hessian = apply_backward(sens_tiles, image_half, row_slots, col_onehot)
-        hessian = lax.psum(partial_hessian, "rows")
+        hessian = node_time(partial_hessian, "rows")
         whole_result = factor_whole(hessian, total)
         basis_now = whole_result.astype(jnp.bfloat16)
         result = lax.dynamic_slice_in_dim(

time: 663 us -> 733 us (1.11)
  waiting for transfers between devices: 197 us -> 252 us
  starting transfers between devices: 0.13 us -> 18.2 us
  other arithmetic: 51.9 us -> 66.6 us
  between operations: 14.7 us -> 1.61 us
  blocking collectives: 201 us -> 213 us
  matrix products: 151 us -> 140 us
    ppermute x0 -> x8, waiting for transfers between devices: none -> 252 us  [node_time(): d_next = ppermute(parts_out, mesh_name, left_arr)]
    psum x4 -> x0, waiting for transfers between devices: 197 us -> none  [local(): hessian = lax.psum(partial_hessian, 'rows')]
    ppermute x0 -> x8, starting transfers between devices: none -> 18.2 us  [node_time(): d_next = ppermute(parts_out, mesh_name, left_arr)]
    add x0 -> x8, other arithmetic: none -> 14.7 us  [node_time(): parts_out = parts_out + d_next]
    psum x4, blocking collectives: 96.9 us -> 108 us  [factor_whole(): gram = lax.psum(local_gram, 'blk') / total]
  transfers between devices with their start and end apart: 4 -> 8, of which waited for: 4 -> 8; matrix products, arithmetic and copies ran while one was open for 0% -> 0% of each run, Pallas kernels for 0% -> 0%
where the time goes in v1:
time: 733 us; the launch traced here: 724 us
  waiting for transfers between devices  252 us (34%)
  blocking collectives  213 us (29%)
  matrix products  140 us (19%)
  other arithmetic  66.6 us (9%)
  local copies, waits for them, and re-layouts  33.5 us (5%)
  starting transfers between devices  18.2 us (2%)
    ppermute x8, waiting for transfers between devices, node_time(): d_next = ppermute(parts_out, mesh_name, left_arr)  252 us
    psum x4, blocking collectives, factor_whole(): gram = lax.psum(local_gram, 'blk') / total  108 us
    psum x4, blocking collectives, local(): image = lax.psum(partial_image, 'blk')  104 us
    dot_general x4, matrix products, apply_forward(): jnp.einsum('kst,sit->ksi', picked, sens_tiles, preferred_element_type=jnp...  41.5 us
    dot_general x4, matrix products, apply_forward(): jnp.einsum('ksi,rs->kri', products, row_onehot, precision=lax.Precision.H...  31 us
    dot_general x4, matrix products, apply_backward(): jnp.einsum('ksj,cs->kcj', products, col_onehot, precision=lax.Precision.H...  30.9 us
    dot_general x4, matrix products, apply_backward(): jnp.einsum('ksi,sij->ksj', picked, sens_tiles, preferred_element_type=jnp...  28.1 us
    another operation x12, other arithmetic, factor_whole(): lower = jnp.linalg.cholesky(gram)  26.1 us
  transfers between devices with their start and end apart: 8, of which 8 were waited for; matrix products, arithmetic and copies ran while one was open for 0% of the time, Pallas kernels for 0%

profile of v1, /device:TPU:0, one launch (start us, length us, event | category | flops | bytes accessed | tf_op | source)
XLA Modules:
  0.0 724.2 jit_solution(9180322870415601021)
XLA Ops:
  6.0 10.4 %fusion.48 = f32[64,256,128]{2,0,1:T(8,128)S(1)} fusion(bf16[256,128,128]{2,1,0:T(8,128)(2,1)} %param.12, bf16[256,64,128]{2,1,0:T(8,128)(2,1)} %gather_fusion, pred[256]{0:T(512)(128)(4,1)S(1)} %get-tuple-element.8), kind=kOutput, calls=%fused_computation.56 | convolution fusion | flops 538968064 | bytes 20971776 | tf_op jit(solution)/shard_map/kst,sit->ksi/dot_general | solution.py:27
  24.2 28.4 %all-reduce.4 = bf16[64,1024]{1,0:T(8,128)(2,1)S(1)} all-reduce(f32[64,1024]{1,0:T(8,128)S(1)} %bitcast.248), channel_id=1, replica_groups=mesh['blk'=8,'rows'=4] {'blk'}, use_global_device_ids=true, to_apply=%region_0.0 | all-reduce | flops 65536 | bytes 393216 | tf_op jit(solution)/shard_map/psum | solution.py:67
  72.7 20.8 %collective-permute-done = f32[64,4096]{1,0:T(8,128)S(1)} collective-permute-done((f32[64,4096]{1,0:T(8,128)S(1)}, f32[64,4096]{1,0:T(8,128)S(1)}, u32[]{:S(2)}, u32[]{:S(2)}) %collective-permute-start) | collective-permute-done | bytes 1048608 | tf_op jit(solution)/shard_map/ppermute | solution.py:18
  93.5 10.4 %fusion.116 = f32[64,4096]{1,0:T(8,128)S(1)} fusion(f32[64,4096]{1,0:T(8,128)S(1)} %collective-permute-done, f32[8,8,32,128]{3,2,1,0:T(8,128)S(1)} %bitcast.235), kind=kLoop, calls=%fused_computation.159 | loop fusion | flops 262144 | bytes 3145728 | tf_op jit(solution)/shard_map/add | solution.py:19
  106.5 42.2 %collective-permute-done.1 = f32[64,4096]{1,0:T(8,128)S(1)} collective-permute-done((f32[64,4096]{1,0:T(8,128)S(1)}, f32[64,4096]{1,0:T(8,128)S(1)}, u32[]{:S(2)}, u32[]{:S(2)}) %collective-permute-start.1) | collective-permute-done | bytes 1048608 | tf_op jit(solution)/shard_map/ppermute | solution.py:18
  149.9 27.9 %psum.57 = f32[64,64]{0,1:T(8,128)S(1)} all-reduce(f32[64,64]{0,1:T(8,128)S(1)} %fusion.120), channel_id=1, replica_groups=mesh['blk'=8,'rows'=4] {'blk'}, use_global_device_ids=true, to_apply=%region_1.0 | all-reduce | flops 4096 | bytes 32768 | tf_op jit(solution)/shard_map/psum | solution.py:43
  195.1 10.4 %fusion.54 = f32[64,256,128]{2,0,1:T(8,128)S(1)} fusion(bf16[256,128,128]{2,1,0:T(8,128)(2,1)} %param.12, bf16[256,64,128]{2,1,0:T(8,128)(2,1)} %gather_fusion.2, pred[256]{0:T(512)(128)(4,1)S(1)} %get-tuple-element.8), kind=kOutput, calls=%fused_computation.58 | convolution fusion | flops 538968064 | bytes 20971776 | tf_op jit(solution)/shard_map/kst,sit->ksi/dot_general | solution.py:27
  205.5 7.9 %fusion.10 = f32[8,64,128]{2,0,1:T(8,128)S(1)} fusion(f32[64,256,128]{2,0,1:T(8,128)S(1)} %fusion.54, s32[256]{0:T(256)S(1)} %bitcast.255, pred[256]{0:T(512)(128)(4,1)S(1)} %iota_compare_fusion.4), kind=kOutput, calls=%fused_computation.18 | convolution fusion | flops 201330688 | bytes 8652032 | tf_op jit(solution)/shard_map/ksi,rs->kri/dot_general | solution.py:28
  213.4 25.5 %all-reduce.5 = bf16[64,1024]{1,0:T(8,128)(2,1)S(1)} all-reduce(f32[64,1024]{1,0:T(8,128)S(1)} %bitcast.249), channel_id=1, replica_groups=mesh['blk'=8,'rows'=4] {'blk'}, use_global_device_ids=true, to_apply=%region_4.9 | all-reduce | flops 65536 | bytes 393216 | tf_op jit(solution)/shard_map/psum | solution.py:67
  258.9 20.9 %collective-permute-done.2 = f32[64,4096]{1,0:T(8,128)S(1)} collective-permute-done((f32[64,4096]{1,0:T(8,128)S(1)}, f32[64,4096]{1,0:T(8,128)S(1)}, u32[]{:S(2)}, u32[]{:S(2)}) %collective-permute-start.2) | collective-permute-done | bytes 1048608 | tf_op jit(solution)/shard_map/ppermute | solution.py:18
  283.9 42.6 %collective-permute-done.3 = f32[64,4096]{1,0:T(8,128)S(1)} collective-permute-done((f32[64,4096]{1,0:T(8,128)S(1)}, f32[64,4096]{1,0:T(8,128)S(1)}, u32[]{:S(2)}, u32[]{:S(2)}) %collective-permute-start.3) | collective-permute-done | bytes 1048608 | tf_op jit(solution)/shard_map/ppermute | solution.py:18
  327.5 27.3 %psum.59 = f32[64,64]{0,1:T(8,128)S(1)} all-reduce(f32[64,64]{0,1:T(8,128)S(1)} %fusion.121), channel_id=1, replica_groups=mesh['blk'=8,'rows'=4] {'blk'}, use_global_device_ids=true, to_apply=%region_5.10 | all-reduce | flops 4096 | bytes 32768 | tf_op jit(solution)/shard_map/psum | solution.py:43
  372.2 10.4 %fusion.60 = f32[64,256,128]{2,0,1:T(8,128)S(1)} fusion(bf16[256,128,128]{2,1,0:T(8,128)(2,1)} %param.12, bf16[256,64,128]{2,1,0:T(8,128)(2,1)} %gather_fusion.4, pred[256]{0:T(512)(128)(4,1)S(1)} %get-tuple-element.8), kind=kOutput, calls=%fused_computation.60 | convolution fusion | flops 538968064 | bytes 20971776 | tf_op jit(solution)/shard_map/kst,sit->ksi/dot_general | solution.py:27
  382.6 7.9 %fusion.6 = f32[8,64,128]{2,0,1:T(8,128)S(1)} fusion(f32[64,256,128]{2,0,1:T(8,128)S(1)} %fusion.60, s32[256]{0:T(256)S(1)} %bitcast.256, pred[256]{0:T(512)(128)(4,1)S(1)} %iota_compare_fusion.4), kind=kOutput, calls=%fused_computation.14 | convolution fusion | flops 201330688 | bytes 8652032 | tf_op jit(solution)/shard_map/ksi,rs->kri/dot_general | solution.py:28
  390.6 25.2 %all-reduce.6 = bf16[64,1024]{1,0:T(8,128)(2,1)S(1)} all-reduce(f32[64,1024]{1,0:T(8,128)S(1)} %bitcast.250), channel_id=1, replica_groups=mesh['blk'=8,'rows'=4] {'blk'}, use_global_device_ids=true, to_apply=%region_6.11 | all-reduce | flops 65536 | bytes 393216 | tf_op jit(solution)/shard_map/psum | solution.py:67
  435.6 21.7 %collective-permute-done.4 = f32[64,4096]{1,0:T(8,128)S(1)} collective-permute-done((f32[64,4096]{1,0:T(8,128)S(1)}, f32[64,4096]{1,0:T(8,128)S(1)}, u32[]{:S(2)}, u32[]{:S(2)}) %collective-permute-start.4) | collective-permute-done | bytes 1048608 | tf_op jit(solution)/shard_map/ppermute | solution.py:18
  461.0 43.0 %collective-permute-done.5 = f32[64,4096]{1,0:T(8,128)S(1)} collective-permute-done((f32[64,4096]{1,0:T(8,128)S(1)}, f32[64,4096]{1,0:T(8,128)S(1)}, u32[]{:S(2)}, u32[]{:S(2)}) %collective-permute-start.5) | collective-permute-done | bytes 1048608 | tf_op jit(solution)/shard_map/ppermute | solution.py:18
  505.1 26.3 %psum.61 = f32[64,64]{0,1:T(8,128)S(1)} all-reduce(f32[64,64]{0,1:T(8,128)S(1)} %fusion.122), channel_id=1, replica_groups=mesh['blk'=8,'rows'=4] {'blk'}, use_global_device_ids=true, to_apply=%region_7.12 | all-reduce | flops 4096 | bytes 32768 | tf_op jit(solution)/shard_map/psum | solution.py:43
  548.7 10.4 %fusion.66 = f32[64,256,128]{2,0,1:T(8,128)S(1)} fusion(bf16[256,128,128]{2,1,0:T(8,128)(2,1)} %param.12, bf16[256,64,128]{2,1,0:T(8,128)(2,1)} %gather_fusion.6, pred[256]{0:T(512)(128)(4,1)S(1)} %get-tuple-element.8), kind=kOutput, calls=%fused_computation.62 | convolution fusion | flops 538968064 | bytes 20971776 | tf_op jit(solution)/shard_map/kst,sit->ksi/dot_general | solution.py:27
  566.9 25.4 %all-reduce.7 = bf16[64,1024]{1,0:T(8,128)(2,1)S(1)} all-reduce(f32[64,1024]{1,0:T(8,128)S(1)} %bitcast.251), channel_id=1, replica_groups=mesh['blk'=8,'rows'=4] {'blk'}, use_global_device_ids=true, to_apply=%region_8.13 | all-reduce | flops 65536 | bytes 393216 | tf_op jit(solution)/shard_map/psum | solution.py:67
  602.3 7.7 %fusion = f32[32,64,128]{2,0,1:T(8,128)S(1)} fusion(f32[64,256,128]{2,0,1:T(8,128)S(1)} %fusion.69, s32[256]{0:T(256)S(1)} %bitcast.263, pred[256]{0:T(512)(128)(4,1)S(1)} %iota_compare_fusion.4), kind=kOutput, calls=%fused_computation.8 | convolution fusion | flops 805322752 | bytes 9438464 | tf_op jit(solution)/shard_map/ksj,cs->kcj/dot_general | solution.py:37
  612.1 21.1 %collective-permute-done.6 = f32[64,4096]{1,0:T(8,128)S(1)} collective-permute-done((f32[64,4096]{1,0:T(8,128)S(1)}, f32[64,4096]{1,0:T(8,128)S(1)}, u32[]{:S(2)}, u32[]{:S(2)}) %collective-permute-start.6) | collective-permute-done | bytes 1048608 | tf_op jit(solution)/shard_map/ppermute | solution.py:18
  640.3 40.0 %collective-permute-done.7 = f32[64,4096]{1,0:T(8,128)} collective-permute-done((f32[64,4096]{1,0:T(8,128)S(1)}, f32[64,4096]{1,0:T(8,128)}, u32[]{:S(2)}, u32[]{:S(2)}) %collective-permute-start.7) | collective-permute-done | bytes 1048608 | tf_op jit(solution)/shard_map/ppermute | solution.py:18
  682.7 26.7 %psum.63 = f32[64,64]{0,1:T(8,128)S(1)} all-reduce(f32[64,64]{0,1:T(8,128)S(1)} %fusion.123), channel_id=1, replica_groups=mesh['blk'=8,'rows'=4] {'blk'}, use_global_device_ids=true, to_apply=%region_9.14 | all-reduce | flops 4096 | bytes 32768 | tf_op jit(solution)/shard_map/psum | solution.py:43
  (113 shorter events, 182.4 us)
Async XLA Ops:
  0.0 2.8 copy-start
  6.0 10.4 %copy-start.5 = (s32[256,1]{0,1:T(1,128)S(1)}, s32[256,1]{0,1:T(1,128)}, u32[]{:S(2)}) copy-start(s32[256,1]{0,1:T(1,128)} %param.14) | copy-start | bytes 3076
  55.7 7.0 copy-start.6
  71.1 22.4 %collective-permute-start = (f32[64,4096]{1,0:T(8,128)S(1)}, f32[64,4096]{1,0:T(8,128)S(1)}, u32[]{:S(2)}, u32[]{:S(2)}) collective-permute-start(f32[64,4096]{1,0:T(8,128)S(1)} %bitcast.244), channel_id=1, source_target_pairs={{0,1},{1,0},{2,3},{3,2},{4,5},{5,4},{6,7},{7,6},{8,9},{9,8},{10,11... | collective-permute-start | bytes 3145736 | tf_op jit(solution)/shard_map/ppermute | solution.py:18
  103.9 44.9 %collective-permute-start.1 = (f32[64,4096]{1,0:T(8,128)S(1)}, f32[64,4096]{1,0:T(8,128)S(1)}, u32[]{:S(2)}, u32[]{:S(2)}) collective-permute-start(f32[64,4096]{1,0:T(8,128)S(1)} %fusion.116), channel_id=1, source_target_pairs={{0,2},{1,3},{2,0},{3,1},{4,6},{5,7},{6,4},{7,5},{8,10},{9,11},{10,... | collective-permute-start | bytes 3145736 | tf_op jit(solution)/shard_map/ppermute | solution.py:18
  191.0 1.0 copy-start.2
  257.3 22.5 %collective-permute-start.2 = (f32[64,4096]{1,0:T(8,128)S(1)}, f32[64,4096]{1,0:T(8,128)S(1)}, u32[]{:S(2)}, u32[]{:S(2)}) collective-permute-start(f32[64,4096]{1,0:T(8,128)S(1)} %bitcast.245), channel_id=1, source_target_pairs={{0,1},{1,0},{2,3},{3,2},{4,5},{5,4},{6,7},{7,6},{8,9},{9,8},{10,11... | collective-permute-start | bytes 3145736 | tf_op jit(solution)/shard_map/ppermute | solution.py:18
  280.7 45.8 %collective-permute-start.3 = (f32[64,4096]{1,0:T(8,128)S(1)}, f32[64,4096]{1,0:T(8,128)S(1)}, u32[]{:S(2)}, u32[]{:S(2)}) collective-permute-start(f32[64,4096]{1,0:T(8,128)S(1)} %fusion.117), channel_id=1, source_target_pairs={{0,2},{1,3},{2,0},{3,1},{4,6},{5,7},{6,4},{7,5},{8,10},{9,11},{10,... | collective-permute-start | bytes 3145736 | tf_op jit(solution)/shard_map/ppermute | solution.py:18
  368.1 1.0 copy-start.3
  434.2 23.1 %collective-permute-start.4 = (f32[64,4096]{1,0:T(8,128)S(1)}, f32[64,4096]{1,0:T(8,128)S(1)}, u32[]{:S(2)}, u32[]{:S(2)}) collective-permute-start(f32[64,4096]{1,0:T(8,128)S(1)} %bitcast.246), channel_id=1, source_target_pairs={{0,1},{1,0},{2,3},{3,2},{4,5},{5,4},{6,7},{7,6},{8,9},{9,8},{10,11... | collective-permute-start | bytes 3145736 | tf_op jit(solution)/shard_map/ppermute | solution.py:18
  458.1 45.9 %collective-permute-start.5 = (f32[64,4096]{1,0:T(8,128)S(1)}, f32[64,4096]{1,0:T(8,128)S(1)}, u32[]{:S(2)}, u32[]{:S(2)}) collective-permute-start(f32[64,4096]{1,0:T(8,128)S(1)} %fusion.118), channel_id=1, source_target_pairs={{0,2},{1,3},{2,0},{3,1},{4,6},{5,7},{6,4},{7,5},{8,10},{9,11},{10,... | collective-permute-start | bytes 3145736 | tf_op jit(solution)/shard_map/ppermute | solution.py:18
  544.6 1.0 copy-start.4
  610.7 22.6 %collective-permute-start.6 = (f32[64,4096]{1,0:T(8,128)S(1)}, f32[64,4096]{1,0:T(8,128)S(1)}, u32[]{:S(2)}, u32[]{:S(2)}) collective-permute-start(f32[64,4096]{1,0:T(8,128)S(1)} %bitcast.247), channel_id=1, source_target_pairs={{0,1},{1,0},{2,3},{3,2},{4,5},{5,4},{6,7},{7,6},{8,9},{9,8},{10,11... | collective-permute-start | bytes 3145736 | tf_op jit(solution)/shard_map/ppermute | solution.py:18
  634.2 46.2 %collective-permute-start.7 = (f32[64,4096]{1,0:T(8,128)S(1)}, f32[64,4096]{1,0:T(8,128)}, u32[]{:S(2)}, u32[]{:S(2)}) collective-permute-start(f32[64,4096]{1,0:T(8,128)S(1)} %fusion.119), channel_id=1, source_target_pairs={{0,2},{1,3},{2,0},{3,1},{4,6},{5,7},{6,4},{7,5},{8,10},{9,11},{10,... | collective-permute-start | bytes 3145736 | tf_op jit(solution)/shard_map/ppermute | solution.py:18
  680.3 43.4 %copy-start.1 = (bf16[64,4096]{1,0:T(8,128)(2,1)S(1)}, bf16[64,4096]{1,0:T(8,128)(2,1)}, u32[]{:S(2)}) copy-start(bf16[64,4096]{1,0:T(8,128)(2,1)} %param.13) | copy-start | bytes 1572868
